TPU v7x, 256 devices: a whole 4x4x8 slice. The times are simulated.
256 devices in a mesh: space: 64 (over x, z, core), slab: 4 (over y).
Axes of the slice: x: 4, y: 4, z: 8, core: 2. Of those that a mesh axis runs over, the one named last changes fastest.
Arguments:
- tokens: float32 [65536, 512], P(('space', 'slab')), may hold values from -6 to 6
- gain: float32 [512], replicated, may hold values from 0.25 to 1.75
- query_weight: float32 [512, 512], replicated, may hold values from -3.1 to 3.1
- key_weight: float32 [512, 512], replicated, may hold values from -0.25 to 0.25
- value_weight: float32 [512, 512], replicated, may hold values from -0.25 to 0.25
- output_weight: float32 [512, 512], replicated, may hold values from -0.25 to 0.25
- neighbour_list: int32 [512, 3], P(('space', 'slab')), may hold values from 0 to 5, as said below
- neighbour_count: int32 [512], P(('space', 'slab')), may hold values from 1 to 3, as said below
- cotangent: float32 [65536, 512], P(('space', 'slab')), may hold values from -6 to 6
Outputs:
- result: float32 [65536, 512], P(('space', 'slab'))
- d_tokens: float32 [65536, 512], P(('space', 'slab'))
- d_gain: float32 [512], replicated
- d_query: float32 [512, 512], replicated
- d_key: float32 [512, 512], replicated
- d_value: float32 [512, 512], replicated
- d_output: float32 [512, 512], replicated
Inputs may be any that keep to these rules, and one draw needn't show every extreme that they name: `neighbour_list`: each row holds distinct window indices, never the patch's own index 2 + p % 2. Only the first neighbour_count[p] entries of a row are live.
All inputs are finite; a program needn't handle non-finite values.
Results may differ from a plain program's by a relative error of at most 0.0003.
Values sent between devices are 32-bit elements; how exact they have to be, the bound alone decides.
A program may use at most 128 MiB of HBM per device.

v0:
```python
import jax
import jax.numpy as jnp
from jax import lax
from jax.sharding import PartitionSpec as P

HEADS = 8
PT = 128


def extended(cells, sides, width):
    for axis, dim in sides:
        count = lax.axis_size(axis)
        head = lax.slice_in_dim(cells, 0, width, axis=dim)
        tail = lax.slice_in_dim(cells, cells.shape[dim] - width, cells.shape[dim], axis=dim)
        cells = jnp.concatenate(
            [
                lax.ppermute(tail, axis, [(i, (i + 1) % count) for i in range(count)]),
                cells,
                lax.ppermute(head, axis, [((i + 1) % count, i) for i in range(count)]),
            ],
            axis=dim,
        )
    return cells


def passed_along(value, axis, steps):
    count = lax.axis_size(axis)
    pairs = [(source, (source + steps) % count) for source in range(count)]
    return lax.ppermute(value, axis, pairs)


def matmul(left, right):
    return jnp.dot(left, right, precision=lax.Precision.HIGHEST, preferred_element_type=jnp.float32)


def normalize(tokens, gain):
    row_mean = jnp.mean(tokens, axis=1, keepdims=True)
    centred = tokens - row_mean
    variance = jnp.mean(centred * centred, axis=1, keepdims=True)
    return centred * lax.rsqrt(variance + 1e-05) * gain[None, :]


def attention(query, key_win, value_win, block_index, live_mask):
    patch_count = block_index.shape[0]
    model_width = query.shape[1]
    head_dim = model_width // HEADS
    picked_keys = key_win.reshape(-1, PT, model_width)[block_index].reshape(
        patch_count, -1, HEADS, head_dim
    )
    picked_values = value_win.reshape(-1, PT, model_width)[block_index].reshape(
        patch_count, -1, HEADS, head_dim
    )
    query_blocks = query.reshape(patch_count, PT, HEADS, head_dim)
    scores = jnp.einsum(
        "pqhd,pkhd->phqk", query_blocks, picked_keys, precision=lax.Precision.HIGHEST
    ) * head_dim ** (-0.5)
    key_mask = jnp.repeat(live_mask, PT, axis=1)
    scores = jnp.where(key_mask[:, None, None, :], scores, -1e30)
    row_max = jnp.max(scores, axis=3, keepdims=True)
    weights = jnp.exp(scores - row_max)
    probability = weights / jnp.sum(weights, axis=3, keepdims=True)
    mixed = jnp.einsum(
        "phqk,pkhd->pqhd", probability, picked_values, precision=lax.Precision.HIGHEST
    )
    return mixed.reshape(patch_count * PT, model_width)


def body(
    tokens,
    gain,
    query_weight,
    key_weight,
    value_weight,
    output_weight,
    neighbour_list,
    neighbour_count,
    cotangent,
):
    row_count = tokens.shape[0]
    model_width = tokens.shape[1]
    patch_count = neighbour_list.shape[0]
    hidden, norm_pull = jax.vjp(normalize, tokens, gain)
    query = matmul(hidden, query_weight)
    own_blocks = patch_count + jnp.arange(patch_count, dtype=jnp.int32)
    block_index = jnp.concatenate([own_blocks[:, None], neighbour_list], axis=1)
    slot_ids = jnp.arange(neighbour_list.shape[1], dtype=jnp.int32)
    live_mask = jnp.concatenate(
        [jnp.ones((patch_count, 1), dtype=bool), slot_ids[None, :] < neighbour_count[:, None]],
        axis=1,
    )
    key_rows = matmul(hidden, key_weight)
    value_rows = matmul(hidden, value_weight)
    window = extended(jnp.concatenate([key_rows, value_rows], axis=1), (("space", 0),), row_count)
    key_win = window[:, :model_width]
    value_win = window[:, model_width:]

    def local_attention(query_rows, key_part, value_part):
        return attention(query_rows, key_part, value_part, block_index, live_mask)

    mixed, attention_pull = jax.vjp(local_attention, query, key_win, value_win)
    result = matmul(mixed, output_weight) + tokens
    grad_output = matmul(mixed.T, cotangent)
    d_mixed = matmul(cotangent, output_weight.T)
    d_queries, d_key_win, d_value_win = attention_pull(d_mixed)
    grad_query = matmul(hidden.T, d_queries)
    d_window = jnp.concatenate([d_key_win, d_value_win], axis=1)
    d_owned = d_window[row_count : 2 * row_count]
    for offset, halo_part in ((-1, d_window[:row_count]), (1, d_window[2 * row_count :])):
        d_owned = d_owned + passed_along(halo_part, "space", offset)
    d_keys = d_owned[:, :model_width]
    d_values = d_owned[:, model_width:]
    grad_key = matmul(hidden.T, d_keys)
    grad_value = matmul(hidden.T, d_values)
    d_hidden = (
        matmul(d_queries, query_weight.T)
        + matmul(d_keys, key_weight.T)
        + matmul(d_values, value_weight.T)
    )
    d_norm, grad_gain = norm_pull(d_hidden)
    d_tokens = d_norm + cotangent
    grad_gain, grad_query, grad_key, grad_value, grad_output = lax.psum(
        (grad_gain, grad_query, grad_key, grad_value, grad_output), ("space", "slab")
    )
    return (result, d_tokens, grad_gain, grad_query, grad_key, grad_value, grad_output)


def solution(mesh):
    return jax.shard_map(
        body,
        mesh=mesh,
        in_specs=(
            P(("space", "slab"), None),
            P(),
            P(),
            P(),
            P(),
            P(),
            P(("space", "slab"), None),
            P(("space", "slab")),
            P(("space", "slab"), None),
        ),
        out_specs=(P(("space", "slab"), None), P(("space", "slab"), None), P(), P(), P(), P(), P()),
        check_vma=False,
    )
```

profile of v0, /device:TPU:8, one launch (start us, length us, event | category | flops | bytes accessed | tf_op | source)
XLA Modules:
  0.0 428.7 jit_solution(7895990466346102938)
XLA Ops:
  15.6 7.5 %collective-permute-start.1 = (f32[256,1024]{1,0:T(8,128)}, f32[256,1024]{1,0:T(8,128)}, u32[]{:S(2)}, u32[]{:S(2)}) collective-permute-start(f32[256,1024]{1,0:T(8,128)} %pad_maximum_fusion.2), channel_id=1, source_target_pairs={{4,0},{8,4},{12,8},{16,12},{20,16},{24,20},{28,24},{32,28},{36,32}... | collective-permute-start | bytes 3145736 | tf_op jit(solution)/shard_map/ppermute | solution.py:19
  23.6 3.9 fusion.55
  35.7 5.2 %collective-permute-done = f32[256,1024]{1,0:T(8,128)} collective-permute-done((f32[256,1024]{1,0:T(8,128)}, f32[256,1024]{1,0:T(8,128)}, u32[]{:S(2)}, u32[]{:S(2)}) %collective-permute-start) | collective-permute-done | bytes 1048608 | tf_op jit(solution)/shard_map/ppermute | solution.py:17
  44.3 3.4 gather_fusion
  47.8 4.9 %reshape.226 = f32[2,512,8,64]{3,2,1,0:T(8,128)} reshape(f32[8,128,512]{2,1,0:T(8,128)} %gather_fusion) | data formatting | bytes 4194304 | tf_op jit(solution)/shard_map/jvp()/reshape | solution.py:50
  52.6 3.8 copy.41
  58.4 4.4 %reshape.227 = f32[2,512,8,64]{3,2,1,0:T(8,128)} reshape(f32[8,128,512]{2,1,0:T(8,128)} %gather_fusion.1) | data formatting | bytes 4194304 | tf_op jit(solution)/shard_map/jvp()/reshape | solution.py:47
  62.8 3.9 copy.40
  66.7 5.7 %fusion.1 = (f32[2,8,128]{2,1,0:T(8,128)S(1)}, f32[2,8,128,512]{3,2,1,0:T(8,128)S(1)}) fusion(pred[2,512]{1,0:T(4,128)(4,1)S(1)} %bitcast.73, f32[2,512,8,64]{1,3,2,0:T(8,128)} %copy.40, f32[2,128,8,64]{1,0,3,2:T(2,128)S(1)} %copy-done.9), kind=kOutput, calls=%fused_computation.15 | convolution fusion | flops 808450048 | bytes 6824960 | tf_op jit(solution)/shard_map/jvp(pqhd,pkhd->phqk)/dot_general | solution.py:54
  73.8 4.4 %fusion.14 = f32[2,512,8,64]{1,3,2,0:T(8,128)} fusion(f32[2,8,128]{2,1,0:T(8,128)S(1)} %fusion.45, f32[2,8,64,128]{3,0,2,1:T(2,128)S(1)} %bitcast.71, f32[2,8,128,512]{3,2,1,0:T(8,128)S(1)} %get-tuple-element.25, f32[2,8,128]{2,1,0:T(8,128)S(1)} %get-tuple-element.24, pred[2,512]{1,0:T(4,128)(4,1)S(1)} %bitcast.75), kind=kOutput, calls=%fused_computation.30 | convolution fusion | flops 809500672 | bytes 6833152 | tf_op jit(solution)/shard_map/transpose(jvp(phqk,pkhd->pqhd))/dot_general | solution.py:62
  78.2 5.6 %convert_reduce_fusion = (f32[2,8,128]{2,1,0:T(8,128)S(1)}, pred[2,8,128,512]{3,2,1,0:T(32,128)(4,1)S(1)}, f32[2,8,128]{2,1,0:T(8,128)S(1)}, f32[2,8,128,512]{3,2,1,0:T(8,128)S(1)}) fusion(f32[2,8,128]{2,1,0:T(8,128)S(1)} %get-tuple-element.24, f32[2,8,128,512]{3,2,1,0:T(8,128)S(1)} %get-tuple-element.25, pred[2,512]{1,0:T(4,128)(4,1)S(1)} %bitcast.76, ...), kind=kOutput, calls=%fused_computation.5 | convolution fusion | flops 814739456 | bytes 12092416 | tf_op jit(solution)/shard_map/transpose(jvp(phqk,pkhd->pqhd))/dot_general | solution.py:62
  88.0 4.6 %fusion.15 = f32[2,512,8,64]{1,3,2,0:T(8,128)} fusion(f32[2,8,128,512]{3,2,1,0:T(8,128)S(1)} %get-tuple-element.16, pred[2,8,128,512]{3,2,1,0:T(32,128)(4,1)S(1)} %get-tuple-element.18, f32[2,8,128]{2,1,0:T(8,128)S(1)} %negate_divide_fusion, pred[2,512]{1,0:T(4,128)(4,1)S(1)} %bitcast.78, f32[2,128,8,64]{1,0,3,2:T(2,128)S(1)} %copy-done.9), kind=kOutput, calls=%fused_computation.31 | convolution fusion | flops 809500672 | bytes 7873536 | tf_op jit(solution)/shard_map/transpose(jvp(pqhd,pkhd->phqk))/dot_general | solution.py:54
  92.6 3.8 copy.56
  96.5 4.8 %reshape.224 = f32[8,128,512]{2,1,0:T(8,128)} reshape(f32[2,512,8,64]{3,2,1,0:T(8,128)} %copy.56) | data formatting | bytes 4194304 | tf_op jit(solution)/shard_map/transpose(jvp())/reshape | solution.py:47
  101.3 3.8 copy.57
  105.1 4.8 %reshape.225 = f32[8,128,512]{2,1,0:T(8,128)} reshape(f32[2,512,8,64]{3,2,1,0:T(8,128)} %copy.57) | data formatting | bytes 4194304 | tf_op jit(solution)/shard_map/transpose(jvp())/reshape | solution.py:50
  111.3 5.0 %scatter_fusion = f32[6,128,512]{2,1,0:T(8,128)} fusion(f32[6,128,512]{2,1,0:T(8,128)} %broadcast.104.clone, s32[8]{0:T(128)S(1)} %reshape.186, f32[8,128,512]{2,1,0:T(8,128)} %reshape.224), kind=kCustom, calls=%fused_computation.2 | custom fusion | flops 524288 | bytes 6291488 | tf_op jit(solution)/shard_map/transpose(jvp())/scatter-add | solution.py:47
  116.5 3.4 scatter_fusion.1
  121.6 5.0 %collective-permute-start.2 = (f32[256,1024]{1,0:T(8,128)S(1)}, f32[256,1024]{1,0:T(8,128)S(1)}, u32[]{:S(2)}, u32[]{:S(2)}) collective-permute-start(f32[256,1024]{1,0:T(8,128)S(1)} %get-tuple-element.20), channel_id=1, source_target_pairs={{0,252},{4,0},{8,4},{12,8},{16,12},{20,16},{24,20},{28,24},{32,28}... | collective-permute-start | bytes 3145736 | tf_op jit(solution)/shard_map/ppermute | solution.py:29
  126.6 6.9 %fusion.16 = f32[2,128,8,64]{1,3,2,0:T(8,128)S(1)} fusion(f32[2,512,8,64]{1,3,2,0:T(8,128)} %copy.41, f32[2,8,128]{2,1,0:T(8,128)S(1)} %fusion.45, f32[2,8,128,512]{3,2,1,0:T(8,128)S(1)} %copy-done.5, f32[2,8,128]{2,1,0:T(8,128)S(1)} %get-tuple-element.24, pred[2,512]{1,0:T(4,128)(4,1)S(1)} %bitcast.79), kind=kOutput, calls=%fused_computation.32 | convolution fusion | flops 809500672 | bytes 6833152 | tf_op jit(solution)/shard_map/jvp(phqk,pkhd->pqhd)/dot_general | solution.py:62
  134.0 5.6 %fusion.17 = f32[2,128,8,64]{1,3,2,0:T(8,128)S(1)} fusion(f32[2,512,8,64]{1,3,2,0:T(8,128)S(1)} %copy-done.6, f32[2,8,128,512]{3,2,1,0:T(8,128)S(1)} %copy-done.3, pred[2,8,128,512]{3,2,1,0:T(32,128)(4,1)S(1)} %copy-done.17, f32[2,8,128]{2,1,0:T(8,128)S(1)} %negate_divide_fusion, pred[2,512]{1,0:T(4,128)(4,1)S(1)} %bitcast.80), kind=kOutput, calls=%fused_computation.36 | convolution fusion | flops 809500672 | bytes 7873536 | tf_op jit(solution)/shard_map/transpose(jvp(pqhd,pkhd->phqk))/dot_general | solution.py:54
  150.6 3.6 fusion.24
  160.3 72.0 %psum.35 = f32[512]{0:T(512)} all-reduce(f32[512]{0:T(512)S(1)} %get-tuple-element.7), channel_id=1, replica_groups=mesh['space'=64,'slab'=4] {'space','slab'}, use_global_device_ids=true, to_apply=%region_12.13 | all-reduce | flops 512 | bytes 4096 | tf_op jit(solution)/shard_map/psum | solution.py:121
  234.5 180.3 %all-reduce.4.cloned.1.call-done = (f32[512,512]{1,0:T(8,128)}, f32[512,512]{1,0:T(8,128)}, f32[512,512]{1,0:T(8,128)}, f32[512,512]{1,0:T(8,128)}) async-done(((f32[512,512]{1,0:T(8,128)}, f32[512,512]{1,0:T(8,128)}, f32[512,512]{1,0:T(8,128)}, f32[512,512]{1,0:T(8,128)}), (f32[512,512]{1,0:T(8,128)}, f32[512,512]{1,0:T(8,128)}, f32[512,512]{1,0:T(8,128)}, ...) | async-done | bytes 4194320 | tf_op jit(solution)/shard_map/psum | solution.py:121
  (107 shorter events, 57.4 us)
Async XLA Ops:
  7.2 16.4 %copy-start.1 = (f32[256,512]{1,0:T(8,128)S(1)}, f32[256,512]{1,0:T(8,128)}, u32[]{:S(2)}) copy-start(f32[256,512]{1,0:T(8,128)} %param.9) | copy-start | bytes 1572868
  7.2 16.4 %copy-start.23 = (f32[512]{0:T(512)S(1)}, f32[512]{0:T(512)}, u32[]{:S(2)}) copy-start(f32[512]{0:T(512)} %param.10) | copy-start | bytes 6148
  7.2 16.0 %copy-start.24 = (s32[2,3]{1,0:T(2,128)S(1)}, s32[2,3]{1,0:T(2,128)}, u32[]{:S(2)}) copy-start(s32[2,3]{1,0:T(2,128)} %param.15) | copy-start | bytes 76
  7.2 16.2 %copy-start.25 = (s32[2]{0:T(128)S(1)}, s32[2]{0:T(128)}, u32[]{:S(2)}) copy-start(s32[2]{0:T(128)} %param.16) | copy-start | bytes 28
  7.2 407.6 %all-reduce.4.cloned.1.call-start = ((), (), s32[]{:S(2)}) async-start(), calls=%async_computation | async-start | bytes 8388608 | tf_op jit(solution)/shard_map/psum | solution.py:121
  12.0 17.7 %copy-start.13 = (f32[256,512]{1,0:T(8,128)S(1)}, f32[256,512]{1,0:T(8,128)}, u32[]{:S(2)}) copy-start(f32[256,512]{1,0:T(8,128)} %param.17) | copy-start | bytes 1572868
  15.6 20.1 %collective-permute-start.1 = (f32[256,1024]{1,0:T(8,128)}, f32[256,1024]{1,0:T(8,128)}, u32[]{:S(2)}, u32[]{:S(2)}) collective-permute-start(f32[256,1024]{1,0:T(8,128)} %pad_maximum_fusion.2), channel_id=1, source_target_pairs={{4,0},{8,4},{12,8},{16,12},{20,16},{24,20},{28,24},{32,28},{36,32}... | collective-permute-start | bytes 3145736 | tf_op jit(solution)/shard_map/ppermute | solution.py:19
  23.1 17.9 %collective-permute-start = (f32[256,1024]{1,0:T(8,128)}, f32[256,1024]{1,0:T(8,128)}, u32[]{:S(2)}, u32[]{:S(2)}) collective-permute-start(f32[256,1024]{1,0:T(8,128)} %pad_maximum_fusion.2), channel_id=1, source_target_pairs={{0,4},{4,8},{8,12},{12,16},{16,20},{20,24},{24,28},{28,32},{32,36}... | collective-permute-start | bytes 3145736 | tf_op jit(solution)/shard_map/ppermute | solution.py:17
  66.7 7.1 %copy-start.22 = (f32[2,128,8,64]{1,0,3,2:T(2,128)S(1)}, f32[2,128,8,64]{1,0,3,2:T(2,128)}, u32[]{:S(2)}) copy-start(f32[2,128,8,64]{1,0,3,2:T(2,128)} %reshape.178) | copy-start | bytes 1572868
  72.4 11.4 %copy-start.4 = (f32[2,8,128,512]{3,2,1,0:T(8,128)}, f32[2,8,128,512]{3,2,1,0:T(8,128)S(1)}, u32[]{:S(2)}) copy-start(f32[2,8,128,512]{3,2,1,0:T(8,128)S(1)} %get-tuple-element.25) | copy-start | bytes 12582916
  119.9 6.7 %copy-start.5 = (f32[2,8,128,512]{3,2,1,0:T(8,128)S(1)}, f32[2,8,128,512]{3,2,1,0:T(8,128)}, u32[]{:S(2)}) copy-start(f32[2,8,128,512]{3,2,1,0:T(8,128)} %copy-done.4) | copy-start | bytes 12582916
  121.4 23.5 %collective-permute-start.3 = (f32[256,1024]{1,0:T(8,128)S(1)}, f32[256,1024]{1,0:T(8,128)S(1)}, u32[]{:S(2)}, u32[]{:S(2)}) collective-permute-start(f32[256,1024]{1,0:T(8,128)S(1)} %get-tuple-element.21), channel_id=1, source_target_pairs={{0,4},{4,8},{8,12},{12,16},{16,20},{20,24},{24,28},{28,32},{32,36}... | collective-permute-start | bytes 3145736 | tf_op jit(solution)/shard_map/ppermute | solution.py:29
  121.5 12.4 %copy-start.3 = (f32[2,8,128,512]{3,2,1,0:T(8,128)S(1)}, f32[2,8,128,512]{3,2,1,0:T(8,128)}, u32[]{:S(2)}) copy-start(f32[2,8,128,512]{3,2,1,0:T(8,128)} %copy-done.2) | copy-start | bytes 12582916
  121.5 12.4 %copy-start.6 = (f32[2,512,8,64]{1,3,2,0:T(8,128)S(1)}, f32[2,512,8,64]{1,3,2,0:T(8,128)}, u32[]{:S(2)}) copy-start(f32[2,512,8,64]{1,3,2,0:T(8,128)} %copy.40) | copy-start | bytes 6291460
  121.6 12.4 %copy-start.17 = (pred[2,8,128,512]{3,2,1,0:T(32,128)(4,1)S(1)}, pred[2,8,128,512]{3,2,1,0:T(32,128)(4,1)}, u32[]{:S(2)}) copy-start(pred[2,8,128,512]{3,2,1,0:T(32,128)(4,1)} %copy-done.16) | copy-start | bytes 3145732
  121.6 23.4 %collective-permute-start.2 = (f32[256,1024]{1,0:T(8,128)S(1)}, f32[256,1024]{1,0:T(8,128)S(1)}, u32[]{:S(2)}, u32[]{:S(2)}) collective-permute-start(f32[256,1024]{1,0:T(8,128)S(1)} %get-tuple-element.20), channel_id=1, source_target_pairs={{0,252},{4,0},{8,4},{12,8},{16,12},{20,16},{24,20},{28,24},{32,28}... | collective-permute-start | bytes 3145736 | tf_op jit(solution)/shard_map/ppermute | solution.py:29
  134.0 6.0 %copy-start.10 = (f32[2,128,8,64]{1,0,3,2:T(2,128)}, f32[2,128,8,64]{1,0,3,2:T(2,128)S(1)}, u32[]{:S(2)}) copy-start(f32[2,128,8,64]{1,0,3,2:T(2,128)S(1)} %copy.42) | copy-start | bytes 1572868
  134.0 6.0 %copy-start.14 = (f32[256,512]{1,0:T(8,128)S(1)}, f32[256,512]{1,0:T(8,128)}, u32[]{:S(2)}) copy-start(f32[256,512]{1,0:T(8,128)} %param.17) | copy-start | bytes 1572868
  140.0 5.0 %copy-start.12 = (f32[2,128,8,64]{1,0,3,2:T(2,128)}, f32[2,128,8,64]{1,0,3,2:T(2,128)S(1)}, u32[]{:S(2)}) copy-start(f32[2,128,8,64]{1,0,3,2:T(2,128)S(1)} %copy.47) | copy-start | bytes 1572868
  148.4 5.8 %copy-start.11 = (f32[2,128,8,64]{1,0,3,2:T(2,128)S(1)}, f32[2,128,8,64]{1,0,3,2:T(2,128)}, u32[]{:S(2)}) copy-start(f32[2,128,8,64]{1,0,3,2:T(2,128)} %copy-done.10) | copy-start | bytes 1572868
  150.5 6.8 %copy-start.8 = (f32[256,1024]{1,0:T(8,128)S(1)}, f32[256,1024]{1,0:T(8,128)}, u32[]{:S(2)}) copy-start(f32[256,1024]{1,0:T(8,128)} %copy-done.7) | copy-start | bytes 3145732
  150.6 6.8 %copy-start.18 = (f32[512,512]{1,0:T(8,128)S(1)}, f32[512,512]{1,0:T(8,128)}, u32[]{:S(2)}) copy-start(f32[512,512]{1,0:T(8,128)} %param.12) | copy-start | bytes 3145732
  157.3 76.3 %copy-start.15 = (f32[256,512]{1,0:T(8,128)S(1)}, f32[256,512]{1,0:T(8,128)}, u32[]{:S(2)}) copy-start(f32[256,512]{1,0:T(8,128)} %param.17) | copy-start | bytes 1572868
  414.8 5.7 %copy-start.20 = (f32[512,512]{1,0:T(8,128)S(1)}, f32[512,512]{1,0:T(8,128)}, u32[]{:S(2)}) copy-start(f32[512,512]{1,0:T(8,128)} %get-tuple-element.34) | copy-start | bytes 3145732
  (7 other events, 22.0 us)
Sparse Core Ops, SparseCore 0:
  150.7 264.1 all-reduce.3
where the time goes:
time: 436 us; the launch traced here: 429 us
  waiting for transfers between devices  187 us (43%)
  blocking collectives  72 us (17%)
  matrix products  63.4 us (15%)
  local copies, waits for them, and re-layouts  56.7 us (13%)
  other arithmetic  22.6 us (5%)
  between operations  14.9 us (3%)
  starting transfers between devices  12.6 us (3%)
    psum x1, waiting for transfers between devices, body(): lax.psum((grad_gain, grad_query, grad_key, grad_value, grad_output), ('sp...  180 us
    psum x1, blocking collectives, body(): lax.psum((grad_gain, grad_query, grad_key, grad_value, grad_output), ('sp...  72 us
    dot_general x12, matrix products, matmul(): jnp.dot(left, right, precision=lax.Precision.HIGHEST, preferred_element_t...  30.5 us
    reshape x4, local copies, waits for them, and re-layouts, attention(): value_win.reshape(-1, PT, model_width)[block_index]  17.3 us
    dot_general x3, matrix products, attention(): jnp.einsum('phqk,pkhd->pqhd', probability, picked_values, precision=lax.P...  17 us
    reshape x4, local copies, waits for them, and re-layouts, attention(): key_win.reshape(-1, PT, model_width)[block_index]  16.9 us
    dot_general x3, matrix products, attention(): jnp.einsum('pqhd,pkhd->phqk', query_blocks, picked_keys, precision=lax.Pr...  15.9 us
    unnamed x58, local copies, waits for them, and re-layouts  8.76 us
  transfers between devices with their start and end apart: 5, of which 3 were waited for; matrix products, arithmetic and copies ran while one was open for 10% of the time, Pallas kernels for 0%

commit v1 on v0

--- a/solution.py
+++ b/solution.py
@@ -118,8 +118,8 @@
     )
     d_norm, grad_gain = norm_pull(d_hidden)
     d_tokens = d_norm + cotangent
-    grad_gain, grad_query, grad_key, grad_value, grad_output = lax.psum(
-        (grad_gain, grad_query, grad_key, grad_value, grad_output), ("space", "slab")
+    grad_gain, grad_query, grad_key, grad_value, grad_output = jax.lax.psum(
+        jax.lax.psum((grad_gain, grad_query, grad_key, grad_value, grad_output), "space"), "slab"
     )
     return (result, d_tokens, grad_gain, grad_query, grad_key, grad_value, grad_output)
 

time: 436 us -> 510 us (1.17)
  blocking collectives: 72 us -> 137 us
  waiting for transfers between devices: 187 us -> 195 us
    psum x1 -> x2, blocking collectives: 72 us -> 137 us  [the longest x1 128 us: body(): jax.lax.psum((grad_gain, grad_query, grad_key, grad_value, grad_output),...]
    psum x1 -> x2, waiting for transfers between devices: 180 us -> 189 us  [the longest x1 189 us: body(): jax.lax.psum((grad_gain, grad_query, grad_key, grad_value, grad_output),...]
  transfers between devices with their start and end apart: 5 -> 6, of which waited for: 3 -> 3; matrix products, arithmetic and copies ran while one was open for 10% -> 8% of each run, Pallas kernels for 0% -> 0%
where the time goes in v1:
time: 510 us; the launch traced here: 502 us
  waiting for transfers between devices  195 us (38%)
  blocking collectives  137 us (27%)
  matrix products  63.1 us (12%)
  local copies, waits for them, and re-layouts  56.7 us (11%)
  other arithmetic  22.6 us (4%)
  between operations  15 us (3%)
  starting transfers between devices  12.9 us (3%)
    psum x1, waiting for transfers between devices, body(): jax.lax.psum((grad_gain, grad_query, grad_key, grad_value, grad_output),...  189 us
    psum x1, blocking collectives, body(): jax.lax.psum((grad_gain, grad_query, grad_key, grad_value, grad_output),...  128 us
    dot_general x12, matrix products, matmul(): jnp.dot(left, right, precision=lax.Precision.HIGHEST, preferred_element_t...  30.3 us
    reshape x4, local copies, waits for them, and re-layouts, attention(): value_win.reshape(-1, PT, model_width)[block_index]  17.3 us
    dot_general x3, matrix products, attention(): jnp.einsum('phqk,pkhd->pqhd', probability, picked_values, precision=lax.P...  17 us
    reshape x4, local copies, waits for them, and re-layouts, attention(): key_win.reshape(-1, PT, model_width)[block_index]  16.9 us
    dot_general x3, matrix products, attention(): jnp.einsum('pqhd,pkhd->phqk', query_blocks, picked_keys, precision=lax.Pr...  15.9 us
  transfers between devices with their start and end apart: 6, of which 3 were waited for; matrix products, arithmetic and copies ran while one was open for 8% of the time, Pallas kernels for 0%

profile of v1, /device:TPU:8, one launch (start us, length us, event | category | flops | bytes accessed | tf_op | source)
XLA Modules:
  0.0 502.5 jit_solution(12090228150470283688)
XLA Ops:
  15.6 7.5 %collective-permute-start.1 = (f32[256,1024]{1,0:T(8,128)}, f32[256,1024]{1,0:T(8,128)}, u32[]{:S(2)}, u32[]{:S(2)}) collective-permute-start(f32[256,1024]{1,0:T(8,128)} %pad_maximum_fusion.2), channel_id=1, source_target_pairs={{4,0},{8,4},{12,8},{16,12},{20,16},{24,20},{28,24},{32,28},{36,32}... | collective-permute-start | bytes 3145736 | tf_op jit(solution)/shard_map/ppermute | solution.py:19
  23.6 3.9 fusion.55
  35.7 5.2 %collective-permute-done = f32[256,1024]{1,0:T(8,128)} collective-permute-done((f32[256,1024]{1,0:T(8,128)}, f32[256,1024]{1,0:T(8,128)}, u32[]{:S(2)}, u32[]{:S(2)}) %collective-permute-start) | collective-permute-done | bytes 1048608 | tf_op jit(solution)/shard_map/ppermute | solution.py:17
  44.3 3.4 gather_fusion
  47.8 4.9 reshape.226
  52.6 3.8 copy.41
  58.4 4.4 reshape.227
  62.8 3.9 copy.40
  66.7 5.7 %fusion.1 = (f32[2,8,128]{2,1,0:T(8,128)S(1)}, f32[2,8,128,512]{3,2,1,0:T(8,128)S(1)}) fusion(pred[2,512]{1,0:T(4,128)(4,1)S(1)} %bitcast.73, f32[2,512,8,64]{1,3,2,0:T(8,128)} %copy.40, f32[2,128,8,64]{1,0,3,2:T(2,128)S(1)} %copy-done.9), kind=kOutput, calls=%fused_computation.15 | convolution fusion | flops 808450048 | bytes 6824960 | tf_op jit(solution)/shard_map/jvp(pqhd,pkhd->phqk)/dot_general | solution.py:54
  73.8 4.5 fusion.14
  78.3 5.6 %convert_reduce_fusion = (f32[2,8,128]{2,1,0:T(8,128)S(1)}, pred[2,8,128,512]{3,2,1,0:T(32,128)(4,1)S(1)}, f32[2,8,128]{2,1,0:T(8,128)S(1)}, f32[2,8,128,512]{3,2,1,0:T(8,128)S(1)}) fusion(f32[2,8,128]{2,1,0:T(8,128)S(1)} %get-tuple-element.28, f32[2,8,128,512]{3,2,1,0:T(8,128)S(1)} %get-tuple-element.29, pred[2,512]{1,0:T(4,128)(4,1)S(1)} %bitcast.76, ...), kind=kOutput, calls=%fused_computation.5 | convolution fusion | flops 814739456 | bytes 12092416 | tf_op jit(solution)/shard_map/transpose(jvp(phqk,pkhd->pqhd))/dot_general | solution.py:62
  88.0 4.6 fusion.15
  92.7 3.8 copy.56
  96.5 4.8 reshape.224
  101.3 3.8 copy.57
  105.1 4.8 reshape.225
  111.4 5.0 %scatter_fusion = f32[6,128,512]{2,1,0:T(8,128)} fusion(f32[6,128,512]{2,1,0:T(8,128)} %broadcast.104.clone, s32[8]{0:T(128)S(1)} %reshape.186, f32[8,128,512]{2,1,0:T(8,128)} %reshape.224), kind=kCustom, calls=%fused_computation.2 | custom fusion | flops 524288 | bytes 6291488 | tf_op jit(solution)/shard_map/transpose(jvp())/scatter-add | solution.py:47
  121.6 5.0 %collective-permute-start.2 = (f32[256,1024]{1,0:T(8,128)S(1)}, f32[256,1024]{1,0:T(8,128)S(1)}, u32[]{:S(2)}, u32[]{:S(2)}) collective-permute-start(f32[256,1024]{1,0:T(8,128)S(1)} %get-tuple-element.24), channel_id=1, source_target_pairs={{0,252},{4,0},{8,4},{12,8},{16,12},{20,16},{24,20},{28,24},{32,28}... | collective-permute-start | bytes 3145736 | tf_op jit(solution)/shard_map/ppermute | solution.py:29
  126.6 6.9 %fusion.16 = f32[2,128,8,64]{1,3,2,0:T(8,128)S(1)} fusion(f32[2,512,8,64]{1,3,2,0:T(8,128)} %copy.41, f32[2,8,128]{2,1,0:T(8,128)S(1)} %fusion.45, f32[2,8,128,512]{3,2,1,0:T(8,128)S(1)} %copy-done.5, f32[2,8,128]{2,1,0:T(8,128)S(1)} %get-tuple-element.28, pred[2,512]{1,0:T(4,128)(4,1)S(1)} %bitcast.79), kind=kOutput, calls=%fused_computation.32 | convolution fusion | flops 809500672 | bytes 6833152 | tf_op jit(solution)/shard_map/jvp(phqk,pkhd->pqhd)/dot_general | solution.py:62
  134.1 5.6 %fusion.17 = f32[2,128,8,64]{1,3,2,0:T(8,128)S(1)} fusion(f32[2,512,8,64]{1,3,2,0:T(8,128)S(1)} %copy-done.6, f32[2,8,128,512]{3,2,1,0:T(8,128)S(1)} %copy-done.3, pred[2,8,128,512]{3,2,1,0:T(32,128)(4,1)S(1)} %copy-done.17, f32[2,8,128]{2,1,0:T(8,128)S(1)} %negate_divide_fusion, pred[2,512]{1,0:T(4,128)(4,1)S(1)} %bitcast.80), kind=kOutput, calls=%fused_computation.36 | convolution fusion | flops 809500672 | bytes 7873536 | tf_op jit(solution)/shard_map/transpose(jvp(pqhd,pkhd->phqk))/dot_general | solution.py:54
  150.9 189.2 %all-reduce.6.cloned.1.call-done = (f32[512,512]{1,0:T(8,128)}, f32[512,512]{1,0:T(8,128)}, f32[512,512]{1,0:T(8,128)}, f32[512,512]{1,0:T(8,128)}) async-done(((f32[512,512]{1,0:T(8,128)}, f32[512,512]{1,0:T(8,128)}, f32[512,512]{1,0:T(8,128)}, f32[512,512]{1,0:T(8,128)}), (f32[512,512]{1,0:T(8,128)}, f32[512,512]{1,0:T(8,128)}, f32[512,512]{1,0:T(8,128)}, ...) | async-done | bytes 4194320 | tf_op jit(solution)/shard_map/psum | solution.py:122
  340.2 3.4 fusion.24
  349.6 127.5 %psum.70 = f32[512]{0:T(512)S(1)} all-reduce(f32[512]{0:T(512)S(1)} %get-tuple-element.7), channel_id=1, replica_groups=mesh['space'=64,'slab'=4] {'space'}, use_global_device_ids=true, to_apply=%region_12.13 | all-reduce | flops 512 | bytes 4096 | tf_op jit(solution)/shard_map/psum | solution.py:122
  477.1 9.2 %psum.71 = f32[512]{0:T(512)} all-reduce(f32[512]{0:T(512)S(1)} %psum.70), channel_id=1, replica_groups=mesh['space'=64,'slab'=4] {'slab'}, use_global_device_ids=true, to_apply=%region_13.14 | all-reduce | flops 512 | bytes 4096 | tf_op jit(solution)/shard_map/psum | solution.py:121
  (111 shorter events, 61.0 us)
Async XLA Ops:
  7.2 16.4 %copy-start.1 = (f32[256,512]{1,0:T(8,128)S(1)}, f32[256,512]{1,0:T(8,128)}, u32[]{:S(2)}) copy-start(f32[256,512]{1,0:T(8,128)} %param.9) | copy-start | bytes 1572868
  7.2 16.4 %copy-start.23 = (f32[512]{0:T(512)S(1)}, f32[512]{0:T(512)}, u32[]{:S(2)}) copy-start(f32[512]{0:T(512)} %param.10) | copy-start | bytes 6148
  7.2 16.0 %copy-start.24 = (s32[2,3]{1,0:T(2,128)S(1)}, s32[2,3]{1,0:T(2,128)}, u32[]{:S(2)}) copy-start(s32[2,3]{1,0:T(2,128)} %param.15) | copy-start | bytes 76
  7.2 16.2 %copy-start.25 = (s32[2]{0:T(128)S(1)}, s32[2]{0:T(128)}, u32[]{:S(2)}) copy-start(s32[2]{0:T(128)} %param.16) | copy-start | bytes 28
  7.2 332.9 %all-reduce.6.cloned.1.call-start = ((), (), s32[]{:S(2)}) async-start(), calls=%async_computation | async-start | bytes 8388608 | tf_op jit(solution)/shard_map/psum | solution.py:122
  12.0 17.7 %copy-start.13 = (f32[256,512]{1,0:T(8,128)S(1)}, f32[256,512]{1,0:T(8,128)}, u32[]{:S(2)}) copy-start(f32[256,512]{1,0:T(8,128)} %param.17) | copy-start | bytes 1572868
  15.6 20.1 %collective-permute-start.1 = (f32[256,1024]{1,0:T(8,128)}, f32[256,1024]{1,0:T(8,128)}, u32[]{:S(2)}, u32[]{:S(2)}) collective-permute-start(f32[256,1024]{1,0:T(8,128)} %pad_maximum_fusion.2), channel_id=1, source_target_pairs={{4,0},{8,4},{12,8},{16,12},{20,16},{24,20},{28,24},{32,28},{36,32}... | collective-permute-start | bytes 3145736 | tf_op jit(solution)/shard_map/ppermute | solution.py:19
  23.1 17.9 %collective-permute-start = (f32[256,1024]{1,0:T(8,128)}, f32[256,1024]{1,0:T(8,128)}, u32[]{:S(2)}, u32[]{:S(2)}) collective-permute-start(f32[256,1024]{1,0:T(8,128)} %pad_maximum_fusion.2), channel_id=1, source_target_pairs={{0,4},{4,8},{8,12},{12,16},{16,20},{20,24},{24,28},{28,32},{32,36}... | collective-permute-start | bytes 3145736 | tf_op jit(solution)/shard_map/ppermute | solution.py:17
  66.7 7.1 %copy-start.22 = (f32[2,128,8,64]{1,0,3,2:T(2,128)S(1)}, f32[2,128,8,64]{1,0,3,2:T(2,128)}, u32[]{:S(2)}) copy-start(f32[2,128,8,64]{1,0,3,2:T(2,128)} %reshape.178) | copy-start | bytes 1572868
  72.4 11.5 %copy-start.4 = (f32[2,8,128,512]{3,2,1,0:T(8,128)}, f32[2,8,128,512]{3,2,1,0:T(8,128)S(1)}, u32[]{:S(2)}) copy-start(f32[2,8,128,512]{3,2,1,0:T(8,128)S(1)} %get-tuple-element.29) | copy-start | bytes 12582916
  119.9 6.7 %copy-start.5 = (f32[2,8,128,512]{3,2,1,0:T(8,128)S(1)}, f32[2,8,128,512]{3,2,1,0:T(8,128)}, u32[]{:S(2)}) copy-start(f32[2,8,128,512]{3,2,1,0:T(8,128)} %copy-done.4) | copy-start | bytes 12582916
  121.5 23.5 %collective-permute-start.3 = (f32[256,1024]{1,0:T(8,128)S(1)}, f32[256,1024]{1,0:T(8,128)S(1)}, u32[]{:S(2)}, u32[]{:S(2)}) collective-permute-start(f32[256,1024]{1,0:T(8,128)S(1)} %get-tuple-element.25), channel_id=1, source_target_pairs={{0,4},{4,8},{8,12},{12,16},{16,20},{20,24},{24,28},{28,32},{32,36}... | collective-permute-start | bytes 3145736 | tf_op jit(solution)/shard_map/ppermute | solution.py:29
  121.6 12.4 %copy-start.3 = (f32[2,8,128,512]{3,2,1,0:T(8,128)S(1)}, f32[2,8,128,512]{3,2,1,0:T(8,128)}, u32[]{:S(2)}) copy-start(f32[2,8,128,512]{3,2,1,0:T(8,128)} %copy-done.2) | copy-start | bytes 12582916
  121.6 12.4 %copy-start.6 = (f32[2,512,8,64]{1,3,2,0:T(8,128)S(1)}, f32[2,512,8,64]{1,3,2,0:T(8,128)}, u32[]{:S(2)}) copy-start(f32[2,512,8,64]{1,3,2,0:T(8,128)} %copy.40) | copy-start | bytes 6291460
  121.6 12.4 %copy-start.17 = (pred[2,8,128,512]{3,2,1,0:T(32,128)(4,1)S(1)}, pred[2,8,128,512]{3,2,1,0:T(32,128)(4,1)}, u32[]{:S(2)}) copy-start(pred[2,8,128,512]{3,2,1,0:T(32,128)(4,1)} %copy-done.16) | copy-start | bytes 3145732
  121.6 23.4 %collective-permute-start.2 = (f32[256,1024]{1,0:T(8,128)S(1)}, f32[256,1024]{1,0:T(8,128)S(1)}, u32[]{:S(2)}, u32[]{:S(2)}) collective-permute-start(f32[256,1024]{1,0:T(8,128)S(1)} %get-tuple-element.24), channel_id=1, source_target_pairs={{0,252},{4,0},{8,4},{12,8},{16,12},{20,16},{24,20},{28,24},{32,28}... | collective-permute-start | bytes 3145736 | tf_op jit(solution)/shard_map/ppermute | solution.py:29
  134.0 6.0 %copy-start.10 = (f32[2,128,8,64]{1,0,3,2:T(2,128)}, f32[2,128,8,64]{1,0,3,2:T(2,128)S(1)}, u32[]{:S(2)}) copy-start(f32[2,128,8,64]{1,0,3,2:T(2,128)S(1)} %copy.42) | copy-start | bytes 1572868
  134.0 6.0 %copy-start.14 = (f32[256,512]{1,0:T(8,128)S(1)}, f32[256,512]{1,0:T(8,128)}, u32[]{:S(2)}) copy-start(f32[256,512]{1,0:T(8,128)} %param.17) | copy-start | bytes 1572868
  150.6 193.0 %copy-start.11 = (f32[2,128,8,64]{1,0,3,2:T(2,128)S(1)}, f32[2,128,8,64]{1,0,3,2:T(2,128)}, u32[]{:S(2)}) copy-start(f32[2,128,8,64]{1,0,3,2:T(2,128)} %copy-done.10) | copy-start | bytes 1572868
  150.6 338.0 %all-reduce.8.cloned.1.call-start = ((), (), s32[]{:S(2)}) async-start(), calls=%async_computation.1 | async-start | bytes 8388608 | tf_op jit(solution)/shard_map/psum | solution.py:121
  340.1 6.5 %copy-start.8 = (f32[256,1024]{1,0:T(8,128)S(1)}, f32[256,1024]{1,0:T(8,128)}, u32[]{:S(2)}) copy-start(f32[256,1024]{1,0:T(8,128)} %copy-done.7) | copy-start | bytes 3145732
  340.2 6.5 %copy-start.18 = (f32[512,512]{1,0:T(8,128)S(1)}, f32[512,512]{1,0:T(8,128)}, u32[]{:S(2)}) copy-start(f32[512,512]{1,0:T(8,128)} %param.12) | copy-start | bytes 3145732
  346.7 141.0 %copy-start.15 = (f32[256,512]{1,0:T(8,128)S(1)}, f32[256,512]{1,0:T(8,128)}, u32[]{:S(2)}) copy-start(f32[256,512]{1,0:T(8,128)} %param.17) | copy-start | bytes 1572868
  488.6 5.7 %copy-start.20 = (f32[512,512]{1,0:T(8,128)S(1)}, f32[512,512]{1,0:T(8,128)}, u32[]{:S(2)}) copy-start(f32[512,512]{1,0:T(8,128)} %get-tuple-element.38) | copy-start | bytes 3145732
  (8 other events, 26.9 us)
Sparse Core Ops, SparseCore 0:
  150.7 189.3 all-reduce.5
  342.8 96.1 all-reduce.7
